TPU v7x, 128 devices: a whole 4x4x4 slice. The times are simulated.
128 devices in a mesh: seq: 16 (over z, x), dp: 8 (over y, core).
Axes of the slice: x: 4, y: 4, z: 4, core: 2. Of those that a mesh axis runs over, the one named last changes fastest.
Arguments:
- query_input: bfloat16 [8, 8192, 2048], P('dp', 'seq'), may hold values from -300 to 300
- key_input: bfloat16 [8, 8192, 2048], P('dp', 'seq'), may hold values from -6 to 6
- value_input: bfloat16 [8, 8192, 2048], P('dp', 'seq'), may hold values from -6 to 6
- keep_blocks: int32 [8, 16], P('dp'), may hold values from 0 to 63, as said below
- dest_slots: int32 [8, 16], P('dp'), may hold values from 0 to 15, each once within a row
- proj_weights: bfloat16 [3, 2048, 2048], P(None, None, 'seq'), may hold values from -5 to 5
- cotangent: bfloat16 [8, 2048, 2048], P('dp', None, 'seq'), may hold values from -6 to 6
Outputs:
- window_out: bfloat16 [8, 8192, 2048], P('dp', 'seq')
- causal_out: bfloat16 [8, 2048, 2048], P('dp', None, 'seq')
- weight_grad: float32 [3, 2048, 2048], P(None, None, 'seq')
- row_grad: bfloat16 [8, 2048, 2048], P('dp', 'seq')
Inputs may be any that keep to these rules, and one draw needn't show every extreme that they name: `keep_blocks`: each row lists 16 distinct block numbers in increasing order, block b covering positions b * 128 to b * 128 + 127. The 4 blocks on one index of seq contribute at most 2 kept blocks, and in every document some index of seq contributes exactly 2. `dest_slots`: each row is a permutation.
All inputs are finite; a program needn't handle non-finite values.
Results may differ from a plain program's by a relative error of at most 0.015.
Values may be sent and summed in bfloat16 or wider, within the bound.
A program may use at most 192 MiB of HBM per device.

v0:
```python
import jax
import jax.numpy as jnp
from jax import lax
from jax.sharding import PartitionSpec as P

HEAD = 128
WIN = 1024
BLK = 128


def passed_along(x, axis, by):
    length = lax.axis_size(axis)
    pairs = [(i, i + by) for i in range(length) if 0 <= i + by < length]
    return lax.ppermute(x, axis, pairs)


def window_head(query_rows, key_rows, value_rows, allowed):
    score_scale = HEAD ** (-0.5)
    scores = (
        lax.dot_general(
            query_rows, key_rows, (((1,), (1,)), ((), ())), preferred_element_type=jnp.float32
        )
        * score_scale
    )
    scores = jnp.where(allowed, scores, -1e30)
    row_max = jnp.max(scores, axis=1, keepdims=True)
    weight = jnp.where(allowed, jnp.exp(scores - row_max), 0.0)
    probabilities = (weight / jnp.sum(weight, axis=1, keepdims=True)).astype(jnp.bfloat16)
    return jnp.dot(probabilities, value_rows, preferred_element_type=jnp.float32).astype(
        jnp.bfloat16
    )


def norm_rows(rows_in):
    values_f = rows_in.astype(jnp.float32)
    mean_square = jnp.mean(values_f * values_f, axis=1, keepdims=True)
    return (values_f * lax.rsqrt(mean_square + 1e-06)).astype(jnp.bfloat16)


def global_head(query_rows, key_rows, value_rows, grad_rows, positions):
    row_count = query_rows.shape[0]
    block_rows = min(512, row_count)
    block_count = row_count // block_rows
    score_scale = HEAD ** (-0.5)

    def step_block(accumulators, block_index):
        key_acc, value_acc = accumulators
        start_row = block_index * block_rows
        query_block = lax.dynamic_slice_in_dim(query_rows, start_row, block_rows, 0)
        grad_block = lax.dynamic_slice_in_dim(grad_rows, start_row, block_rows, 0)
        place_block = lax.dynamic_slice_in_dim(positions, start_row, block_rows, 0)
        causal = positions[None, :] <= place_block[:, None]
        scores = (
            lax.dot_general(
                query_block, key_rows, (((1,), (1,)), ((), ())), preferred_element_type=jnp.float32
            )
            * score_scale
        )
        scores = jnp.where(causal, scores, -1e30)
        row_max = jnp.max(scores, axis=1, keepdims=True)
        weight = jnp.where(causal, jnp.exp(scores - row_max), 0.0)
        soft_weights = weight / jnp.sum(weight, axis=1, keepdims=True)
        probabilities = soft_weights.astype(jnp.bfloat16)
        head_output = jnp.dot(probabilities, value_rows, preferred_element_type=jnp.float32).astype(
            jnp.bfloat16
        )
        d_probs = lax.dot_general(
            grad_block, value_rows, (((1,), (1,)), ((), ())), preferred_element_type=jnp.float32
        )
        value_acc = value_acc + lax.dot_general(
            probabilities, grad_block, (((0,), (0,)), ((), ())), preferred_element_type=jnp.float32
        )
        row_delta = jnp.sum(soft_weights * d_probs, axis=1, keepdims=True)
        d_scores = (soft_weights * (d_probs - row_delta) * score_scale).astype(jnp.bfloat16)
        grad_query = jnp.dot(d_scores, key_rows, preferred_element_type=jnp.float32).astype(
            jnp.bfloat16
        )
        key_acc = key_acc + lax.dot_general(
            d_scores, query_block, (((0,), (0,)), ((), ())), preferred_element_type=jnp.float32
        )
        return ((key_acc, value_acc), (head_output, grad_query))

    zero_acc = jnp.zeros(key_rows.shape, jnp.float32)
    (key_acc, value_acc), (outputs, grad_queries) = lax.scan(
        step_block, (zero_acc, zero_acc), jnp.arange(block_count)
    )
    head_width = query_rows.shape[1]
    return (
        outputs.reshape(row_count, head_width),
        grad_queries.reshape(row_count, head_width),
        key_acc.astype(jnp.bfloat16),
        value_acc.astype(jnp.bfloat16),
    )


def shards(query_input, key_input, value_input, keep_blocks, dest_slots, proj_weights, cotangent):
    query_rows = query_input[0]
    key_rows = key_input[0]
    value_rows = value_input[0]
    tok_rows, feature_width = query_rows.shape
    head_count = feature_width // HEAD
    shard_index = lax.axis_index("seq")
    seq_count = lax.axis_size("seq")
    reach_rows = WIN - 1
    depth_hops = (reach_rows + tok_rows - 1) // tok_rows
    before_keys = []
    before_values = []
    for distance in range(1, depth_hops + 1):
        need_rows = min(tok_rows, reach_rows - (distance - 1) * tok_rows)
        edge_pair = jnp.stack(
            [key_rows[tok_rows - need_rows :], value_rows[tok_rows - need_rows :]]
        )
        arrived = passed_along(edge_pair, "seq", distance)
        before_keys.insert(0, arrived[0])
        before_values.insert(0, arrived[1])
    key_ext = jnp.concatenate(before_keys + [key_rows], axis=0)
    value_ext = jnp.concatenate(before_values + [value_rows], axis=0)
    row_ids = jnp.arange(tok_rows)[:, None]
    col_ids = jnp.arange(tok_rows + reach_rows)[None, :]
    allowed = (
        (col_ids >= row_ids)
        & (col_ids <= row_ids + reach_rows)
        & (col_ids + shard_index * tok_rows >= reach_rows)
    )

    def head_window(head_index):
        column = head_index * HEAD
        return window_head(
            lax.dynamic_slice_in_dim(query_rows, column, HEAD, 1),
            lax.dynamic_slice_in_dim(key_ext, column, HEAD, 1),
            lax.dynamic_slice_in_dim(value_ext, column, HEAD, 1),
            allowed,
        )

    stacked = lax.map(head_window, jnp.arange(head_count))
    window_out = jnp.transpose(stacked, (1, 0, 2)).reshape(tok_rows, feature_width)
    keep_list = keep_blocks[0]
    slot_list = dest_slots[0]
    kept_total = keep_list.shape[0]
    per_shard = tok_rows // BLK
    most_blocks = max(1, per_shard // 2)
    order_inverse = jnp.argsort(slot_list)
    rows_total = kept_total * BLK
    compact_ids = jnp.arange(rows_total, dtype=jnp.int32)
    kept_index = order_inverse[compact_ids // BLK]
    positions = keep_list[kept_index] * BLK + compact_ids % BLK
    local_cols = proj_weights.shape[2]
    wide_weights = jnp.concatenate([proj_weights[0], proj_weights[1], proj_weights[2]], axis=1)
    own_count = rows_total // seq_count
    kept_shard = keep_list // per_shard
    first_kept = jnp.sum(kept_shard < shard_index)
    kept_count = jnp.sum(kept_shard == shard_index)
    slot_ids = jnp.arange(most_blocks)
    pick_index = jnp.minimum(first_kept + slot_ids, kept_total - 1)
    valid_mask = jnp.repeat(slot_ids < kept_count, BLK)
    local_ids = (
        (keep_list[pick_index] % per_shard * BLK)[:, None] + jnp.arange(BLK)[None, :]
    ).reshape(-1)
    packed_rows = norm_rows(jnp.where(valid_mask[:, None], window_out[local_ids], 0))
    shard_piece = lax.all_gather(packed_rows, "seq", axis=0, tiled=True)
    gathered = shard_piece
    projected = jnp.dot(shard_piece, wide_weights, preferred_element_type=jnp.float32).astype(
        jnp.bfloat16
    )
    first_of = jnp.sum(kept_shard[None, :] < kept_shard[:, None], axis=1)
    pack_start = kept_shard * (most_blocks * BLK) + (jnp.arange(kept_total) - first_of) * BLK
    packed_index = pack_start[kept_index] + compact_ids % BLK
    gathered = gathered[packed_index]
    projected = projected[packed_index]
    grad_doc = cotangent[0]
    head_index = 0
    low = head_index * HEAD
    head_result = global_head(
        projected[:, low : low + HEAD],
        projected[:, local_cols + low : local_cols + low + HEAD],
        projected[:, 2 * local_cols + low : 2 * local_cols + low + HEAD],
        grad_doc,
        positions,
    )
    outputs = head_result[0]
    grad_query = head_result[1]
    grad_key = head_result[2]
    grad_value = head_result[3]
    grad_parts = (grad_query, grad_key, grad_value)
    local_grads = jnp.stack(
        [
            lax.dot_general(
                gathered, part, (((0,), (0,)), ((), ())), preferred_element_type=jnp.float32
            )
            for part in grad_parts
        ]
    )
    weight_grad = lax.psum(local_grads.astype(jnp.bfloat16), "dp").astype(jnp.float32)
    term = jnp.zeros((own_count * lax.axis_size("seq"), feature_width), jnp.float32)
    for which_proj in range(3):
        grad_slice = grad_parts[which_proj]
        term = term + lax.dot_general(
            grad_slice,
            proj_weights[which_proj],
            (((1,), (1,)), ((), ())),
            preferred_element_type=jnp.float32,
        )
    row_grad = lax.psum_scatter(term.astype(jnp.bfloat16), "seq", scatter_dimension=0, tiled=True)
    return (window_out[None], outputs[None], weight_grad, row_grad[None])


def solution(mesh):
    return jax.shard_map(
        shards,
        mesh=mesh,
        in_specs=(
            P("dp", "seq", None),
            P("dp", "seq", None),
            P("dp", "seq", None),
            P("dp", None),
            P("dp", None),
            P(None, None, "seq"),
            P("dp", None, "seq"),
        ),
        out_specs=(
            P("dp", "seq", None),
            P("dp", None, "seq"),
            P(None, None, "seq"),
            P("dp", "seq", None),
        ),
        check_vma=False,
    )
```

profile of v0, /device:TPU:0, one launch (start us, length us, event | category | flops | bytes accessed | tf_op | source)
XLA Modules:
  0.0 815.9 jit_solution(6254746076496905836)
XLA Ops:
  9.3 3.2 copy.31
  13.1 5.2 copy.32
  18.3 10.9 %pad_maximum_fusion.1 = bf16[2,511,2048]{2,0,1:T(2,128)(2,1)} fusion(bf16[1,511,2048]{2,0,1:T(2,128)(2,1)} %copy.32, bf16[1,511,2048]{2,0,1:T(2,128)(2,1)S(1)} %copy.31), kind=kLoop, calls=%fused_computation.54 | loop fusion | flops 8372224 | bytes 8372224 | tf_op jit(solution)/shard_map/stack | solution.py:110
  29.2 7.1 collective-permute-start
  38.6 4.7 collective-permute-start.1
  46.1 79.3 %collective-permute-done = bf16[2,511,2048]{2,0,1:T(2,128)(2,1)} collective-permute-done((bf16[2,511,2048]{2,0,1:T(2,128)(2,1)}, bf16[2,511,2048]{2,0,1:T(2,128)(2,1)}, u32[]{:S(2)}, u32[]{:S(2)}) %collective-permute-start) | collective-permute-done | bytes 4186144 | tf_op jit(solution)/shard_map/ppermute | solution.py:14
  125.5 8.7 %fusion.65 = (bf16[1,511,2048]{2,0,1:T(2,128)(2,1)S(1)}, bf16[1,511,2048]{2,0,1:T(2,128)(2,1)S(1)}) fusion(bf16[2,511,2048]{2,0,1:T(2,128)(2,1)} %collective-permute-done), kind=kLoop, calls=%fused_computation.174 | loop fusion | bytes 8372224 | tf_op jit(solution)/shard_map/slice | solution.py:115
  134.1 4.7 copy_bitcast_fusion.1
  138.8 75.4 %collective-permute-done.1 = bf16[2,512,2048]{2,1,0:T(8,128)(2,1)} collective-permute-done((bf16[2,512,2048]{2,1,0:T(8,128)(2,1)}, bf16[2,512,2048]{2,1,0:T(8,128)(2,1)}, u32[]{:S(2)}, u32[]{:S(2)}) %collective-permute-start.1) | collective-permute-done | bytes 4194336 | tf_op jit(solution)/shard_map/ppermute | solution.py:14
  214.2 4.8 slice_bitcast_fusion
  219.0 31.6 %concatenate.10 = bf16[1535,2048]{1,0:T(8,128)(2,1)} concatenate(bf16[511,2048]{1,0:T(8,128)(2,1)} %get-tuple-element.281, bf16[512,2048]{1,0:T(8,128)(2,1)} %get-tuple-element.223, bf16[512,2048]{1,0:T(8,128)(2,1)S(1)} %bitcast.151), dimensions={0} | concatenate | bytes 12574720 | tf_op jit(solution)/shard_map/concatenate | solution.py:117
  250.6 33.6 %concatenate.9 = bf16[1535,2048]{1,0:T(8,128)(2,1)} concatenate(bf16[511,2048]{1,0:T(8,128)(2,1)} %get-tuple-element.282, bf16[512,2048]{1,0:T(8,128)(2,1)} %get-tuple-element.224, bf16[512,2048]{1,0:T(8,128)(2,1)} %bitcast.152), dimensions={0} | concatenate | bytes 12574720 | tf_op jit(solution)/shard_map/concatenate | solution.py:116
  284.2 110.0 %while.28 = (s32[]{:T(128)}, bf16[16,512,128]{2,1,0:T(8,128)(2,1)S(1)}, s32[16]{0:T(128)S(1)}, bf16[512,2048]{1,0:T(8,128)(2,1)}, bf16[1535,2048]{1,0:T(8,128)(2...) while((s32[]{:T(128)}, ...), condition=%wide.region_3.4_spmd.clone, body=%wide.region_0.3_spmd.clone.sunk | while | flops 419745792 | bytes 10504381 | solution.py:135
  404.7 4.3 compare_select_fusion.5
  409.0 5.6 select_select_fusion.1
  414.7 4.5 compare_select_fusion.12
  419.3 5.6 select_select_fusion
  425.0 4.4 compare_select_fusion.11
  429.4 5.5 fusion.51
  437.2 78.3 %all-gather.2.cloned.1.call-done = bf16[4096,2048]{1,0:T(8,128)(2,1)} async-done(((bf16[256,2048]{1,0:T(8,128)(2,1)}), bf16[4096,2048]{1,0:T(8,128)(2,1)}) %all-gather.2.cloned.1.call-update) | async-done | bytes 16777232 | tf_op jit(solution)/shard_map/all_gather | solution.py:160
  515.4 13.7 %convolution_convert_fusion.2 = bf16[4096,384]{1,0:T(8,128)(2,1)} fusion(bf16[4096,2048]{1,0:T(8,128)(2,1)} %all-gather.2.cloned.1.call-done, bf16[2048,128]{1,0:T(8,128)(2,1)S(1)} %get-tuple-element.231, bf16[2048,128]{1,0:T(8,128)(2,1)} %get-tuple-element.232, bf16[2048,128]{1,0:T(8,128)(2,1)S(1)} %get-tuple-element.230), kind=kOutput, calls=%fused_computation.52 | convolution fusion | flops 6448742400 | bytes 21495808 | tf_op jit(solution)/shard_map/dot_general | solution.py:162
  529.1 11.2 %gather_fusion.2 = bf16[2048,384]{1,0:T(8,128)(2,1)} fusion(bf16[4096,384]{1,0:T(8,128)(2,1)} %convolution_convert_fusion.2, s32[2048]{0:T(1024)S(1)} %broadcast_clamp_fusion), kind=kCustom, calls=%fused_computation.2 | custom fusion | bytes 3153920 | tf_op jit(solution)/shard_map/gather | solution.py:169
  542.5 58.0 %while.29 = (s32[]{:T(128)}, f32[2048,128]{1,0:T(8,128)S(1)}, f32[2048,128]{1,0:T(8,128)S(1)}, bf16[4,512,128]{2,1,0:T(8,128)(2,1)}, bf16[4,512,128]{2,1,0:T(8,1...) while((s32[]{:T(128)}, f32[2048,128]{1,0:T(8,128)S(1)}, ...), condition=%wide.region_13.14_spmd.clone, body=%wide.region_9.13_spmd.clone.sunk | while | flops 1636956672 | bytes 55361836 | solution.py:84
  600.4 9.1 %fusion.47 = f32[2048,2048]{1,0:T(8,128)} fusion(f32[2048,128]{1,0:T(8,128)S(1)} %get-tuple-element.106, bf16[3,2048,128]{2,1,0:T(8,128)(2,1)} %param.16), kind=kOutput, calls=%fused_computation.82 | convolution fusion | flops 1074003968 | bytes 18350080 | tf_op jit(solution)/shard_map/dot_general | solution.py:197
  609.5 24.5 %gather_fusion.3 = bf16[2048,2048]{1,0:T(8,128)(2,1)} fusion(bf16[4096,2048]{1,0:T(8,128)(2,1)} %all-gather.2.cloned.1.call-done, s32[2048]{0:T(1024)S(1)} %broadcast_clamp_fusion), kind=kCustom, calls=%fused_computation.3 | custom fusion | bytes 16785408 | tf_op jit(solution)/shard_map/gather | solution.py:168
  634.0 5.9 fusion.36
  642.4 9.1 %fusion.62 = f32[2048,2048]{1,0:T(8,128)} fusion(bf16[2048,128]{1,0:T(8,128)(2,1)S(1)} %bitcast.156, bf16[3,2048,128]{2,1,0:T(8,128)(2,1)} %param.16), kind=kOutput, calls=%fused_computation.172 | convolution fusion | flops 1073741824 | bytes 17825792 | tf_op jit(solution)/shard_map/dot_general | solution.py:197
  655.3 15.8 %add_convert_fusion = bf16[2048,2048]{1,0:T(8,128)(2,1)} fusion(f32[2048,2048]{1,0:T(8,128)} %fusion.62, f32[2048,2048]{1,0:T(8,128)} %fusion.47, f32[2048,128]{1,0:T(8,128)S(1)} %get-tuple-element.107, bf16[3,2048,128]{2,1,0:T(8,128)(2,1)} %param.16), kind=kOutput, calls=%fused_computation.51 | convolution fusion | flops 1086586880 | bytes 43515904 | tf_op jit(solution)/shard_map/dot_general | solution.py:197
  675.4 4.2 broadcast_in_dim_reshape.7
  679.6 39.6 %all-reduce.2.cloned.1.call-done = bf16[3,2048,128]{2,1,0:T(8,128)(2,1)} async-done(((bf16[3,2048,128]{2,1,0:T(8,128)(2,1)}), bf16[3,2048,128]{2,1,0:T(8,128)(2,1)}) %all-reduce.2.cloned.1.call-update) | async-done | bytes 1572880 | tf_op jit(solution)/shard_map/psum | solution.py:193
  719.1 3.3 convert_element_type.59
  722.4 86.5 %reduce-scatter.2.cloned.1.call-done = bf16[128,2048]{1,0:T(8,128)(2,1)} async-done(((bf16[2048,2048]{1,0:T(8,128)(2,1)}), bf16[128,2048]{1,0:T(8,128)(2,1)}) %reduce-scatter.2.cloned.1.call-update) | async-done | bytes 524304 | tf_op jit(solution)/shard_map/reduce_scatter | solution.py:203
  (197 shorter events, 179.6 us)
Async XLA Ops:
  7.2 508.2 %all-gather.2.cloned.1.call-start = ((), (), s32[]{:S(2)}) async-start(), calls=%async_computation.1 | async-start | bytes 17825792 | tf_op jit(solution)/shard_map/all_gather | solution.py:160
  9.3 3.3 copy-start.2
  18.3 18.0 %copy-start.3 = (bf16[1,512,2048]{2,1,0:T(8,128)(2,1)S(1)}, bf16[1,512,2048]{2,1,0:T(8,128)(2,1)}, u32[]{:S(2)}) copy-start(bf16[1,512,2048]{2,1,0:T(8,128)(2,1)} %param.12) | copy-start | bytes 6291460
  29.2 14.1 %copy-start = (s32[1,16]{1,0:T(1,128)S(1)}, s32[1,16]{1,0:T(1,128)}, u32[]{:S(2)}) copy-start(s32[1,16]{1,0:T(1,128)} %param.14) | copy-start | bytes 196
  29.2 96.3 %collective-permute-start = (bf16[2,511,2048]{2,0,1:T(2,128)(2,1)}, bf16[2,511,2048]{2,0,1:T(2,128)(2,1)}, u32[]{:S(2)}, u32[]{:S(2)}) collective-permute-start(bf16[2,511,2048]{2,0,1:T(2,128)(2,1)} %pad_maximum_fusion.1), channel_id=1, source_target_pairs={{0,16},{8,24},{16,32},{24,40},{32,48},{40,56},{48,64},{56,72},{64,... | collective-permute-start | bytes 12558344 | tf_op jit(solution)/shard_map/ppermute | solution.py:14
  38.6 175.6 %collective-permute-start.1 = (bf16[2,512,2048]{2,1,0:T(8,128)(2,1)}, bf16[2,512,2048]{2,1,0:T(8,128)(2,1)}, u32[]{:S(2)}, u32[]{:S(2)}) collective-permute-start(bf16[2,512,2048]{2,1,0:T(8,128)(2,1)} %pad_maximum_fusion), channel_id=1, source_target_pairs={{0,8},{8,16},{16,24},{24,32},{32,40},{40,48},{48,56},{56,64},{64,7... | collective-permute-start | bytes 12582920 | tf_op jit(solution)/shard_map/ppermute | solution.py:14
  250.6 33.6 %copy-start.4 = (bf16[16,512,128]{2,1,0:T(8,128)(2,1)S(1)}, bf16[16,512,128]{2,1,0:T(8,128)(2,1)}, u32[]{:S(2)}) copy-start(bf16[16,512,128]{2,1,0:T(8,128)(2,1)} %custom-call.10) | copy-start | bytes 6291460
  394.2 1.3 copy-start.5
  398.8 1.9 copy-start.10
  400.6 318.5 %all-reduce.2.cloned.1.call-start = ((), (), s32[]{:S(2)}) async-start(), calls=%async_computation.2 | async-start | bytes 3145728 | tf_op jit(solution)/shard_map/psum | solution.py:193
  554.1 1.2 copy-start.7
  557.1 1.0 copy-start.9
  566.5 1.2 copy-start.7
  569.5 1.0 copy-start.9
  578.9 1.2 copy-start.7
  581.9 1.0 copy-start.9
  591.3 1.2 copy-start.7
  594.3 1.0 copy-start.9
  634.0 6.0 copy-start.1
  634.0 6.0 copy-start.8
  655.3 153.7 %reduce-scatter.2.cloned.1.call-start = ((), (), s32[]{:S(2)}) async-start(), calls=%async_computation.3 | async-start | bytes 8912896 | tf_op jit(solution)/shard_map/reduce_scatter | solution.py:203
  671.2 1.6 copy-start.6
Sparse Core Ops, SparseCore 0:
  400.7 114.6 all-gather.1
  655.4 63.6 all-reduce.1
  723.1 85.7 reduce-scatter.1
where the time goes:
time: 828 us; the launch traced here: 816 us
  waiting for transfers between devices  359 us (43%)
  matrix products  165 us (20%)
  local copies, waits for them, and re-layouts  164 us (20%)
  other arithmetic  79.7 us (10%)
  loops' own time  21.7 us (3%)
  between operations  14.5 us (2%)
  starting transfers between devices  11.9 us (1%)
    ppermute x2, waiting for transfers between devices, passed_along(): return lax.ppermute(x, axis, pairs)  155 us
    reduce_scatter x1, waiting for transfers between devices, shards(): lax.psum_scatter(term.astype(jnp.bfloat16), 'seq', scatter_dimension=0, t...  86.5 us
    all_gather x1, waiting for transfers between devices, shards(): shard_piece = lax.all_gather(packed_rows, 'seq', axis=0, tiled=True)  78.3 us
    psum x1, waiting for transfers between devices, shards(): lax.psum(local_grads.astype(jnp.bfloat16), 'dp').astype(jnp.float32)  39.6 us
    dot_general x16, matrix products, window_head(): jnp.dot(probabilities, value_rows, preferred_element_type=jnp.float32)  36.5 us
    dot_general x16, matrix products, window_head(): lax.dot_general(query_rows, key_rows, (((1,), (1,)), ((), ())), preferred...  34.4 us
    dot_general x3, matrix products, shards(): lax.dot_general(grad_slice, proj_weights[which_proj], (((1,), (1,)), ((),...  34 us
    concatenate x1, local copies, waits for them, and re-layouts, shards(): key_ext = jnp.concatenate(before_keys + [key_rows], axis=0)  33.6 us
  transfers between devices with their start and end apart: 5, of which 5 were waited for; matrix products, arithmetic and copies ran while one was open for 10% of the time, Pallas kernels for 0%

commit v1 on v0

--- a/solution.py
+++ b/solution.py
@@ -157,7 +157,15 @@
         (keep_list[pick_index] % per_shard * BLK)[:, None] + jnp.arange(BLK)[None, :]
     ).reshape(-1)
     packed_rows = norm_rows(jnp.where(valid_mask[:, None], window_out[local_ids], 0))
-    shard_piece = lax.all_gather(packed_rows, "seq", axis=0, tiled=True)
+    shard_piece = jnp.concatenate(
+        jax.lax.all_to_all(
+            jnp.stack([packed_rows for _ in range(jax.lax.axis_size("seq"))], 0),
+            "seq",
+            split_axis=0,
+            concat_axis=0,
+        ),
+        0,
+    )
     gathered = shard_piece
     projected = jnp.dot(shard_piece, wide_weights, preferred_element_type=jnp.float32).astype(
         jnp.bfloat16

time: 828 us -> 920 us (1.11)
  waiting for transfers between devices: 359 us -> 440 us
    all_to_all x0 -> x1, waiting for transfers between devices: none -> 214 us  [shards(): jax.lax.all_to_all(jnp.stack([packed_rows for _ in range(jax.lax.axis_siz...]
    all_gather x1 -> x0, waiting for transfers between devices: 78.3 us -> none  [shards(): shard_piece = lax.all_gather(packed_rows, 'seq', axis=0, tiled=True)]
    reduce_scatter x1, waiting for transfers between devices: 86.5 us -> 33.6 us  [shards(): lax.psum_scatter(term.astype(jnp.bfloat16), 'seq', scatter_dimension=0, t...]
  transfers between devices with their start and end apart: 5 -> 5, of which waited for: 5 -> 5; matrix products, arithmetic and copies ran while one was open for 10% -> 9% of each run, Pallas kernels for 0% -> 0%
where the time goes in v1:
time: 920 us; the launch traced here: 908 us
  waiting for transfers between devices  440 us (48%)
  local copies, waits for them, and re-layouts  170 us (18%)
  matrix products  168 us (18%)
  other arithmetic  78.9 us (9%)
  starting transfers between devices  20.7 us (2%)
  between operations  16.1 us (2%)
  loops' own time  13.8 us (2%)
    all_to_all x1, waiting for transfers between devices, shards(): jax.lax.all_to_all(jnp.stack([packed_rows for _ in range(jax.lax.axis_siz...  214 us
    ppermute x2, waiting for transfers between devices, passed_along(): return lax.ppermute(x, axis, pairs)  155 us
    psum x1, waiting for transfers between devices, shards(): lax.psum(local_grads.astype(jnp.bfloat16), 'dp').astype(jnp.float32)  37.7 us
    dot_general x16, matrix products, window_head(): jnp.dot(probabilities, value_rows, preferred_element_type=jnp.float32)  36.5 us
    dot_general x16, matrix products, window_head(): lax.dot_general(query_rows, key_rows, (((1,), (1,)), ((), ())), preferred...  34.4 us
    dot_general x3, matrix products, shards(): lax.dot_general(grad_slice, proj_weights[which_proj], (((1,), (1,)), ((),...  34.1 us
    reduce_scatter x1, waiting for transfers between devices, shards(): lax.psum_scatter(term.astype(jnp.bfloat16), 'seq', scatter_dimension=0, t...  33.6 us
    concatenate x1, local copies, waits for them, and re-layouts, shards(): key_ext = jnp.concatenate(before_keys + [key_rows], axis=0)  33.6 us
  transfers between devices with their start and end apart: 5, of which 5 were waited for; matrix products, arithmetic and copies ran while one was open for 9% of the time, Pallas kernels for 0%

profile of v1, /device:TPU:0, one launch (start us, length us, event | category | flops | bytes accessed | tf_op | source)
XLA Modules:
  0.0 908.3 jit_solution(4047306696298038531)
XLA Ops:
  13.9 5.2 copy.32
  19.1 10.9 %pad_maximum_fusion.1 = bf16[2,511,2048]{2,0,1:T(2,128)(2,1)} fusion(bf16[1,511,2048]{2,0,1:T(2,128)(2,1)} %copy.32, bf16[1,511,2048]{2,0,1:T(2,128)(2,1)S(1)} %copy.31), kind=kLoop, calls=%fused_computation.54 | loop fusion | flops 8372224 | bytes 8372224 | tf_op jit(solution)/shard_map/stack | solution.py:110
  30.0 7.1 collective-permute-start
  39.4 4.6 collective-permute-start.1
  46.8 79.4 %collective-permute-done = bf16[2,511,2048]{2,0,1:T(2,128)(2,1)} collective-permute-done((bf16[2,511,2048]{2,0,1:T(2,128)(2,1)}, bf16[2,511,2048]{2,0,1:T(2,128)(2,1)}, u32[]{:S(2)}, u32[]{:S(2)}) %collective-permute-start) | collective-permute-done | bytes 4186144 | tf_op jit(solution)/shard_map/ppermute | solution.py:14
  126.3 8.7 fusion.65
  134.9 4.7 copy_bitcast_fusion.1
  139.6 75.4 %collective-permute-done.1 = bf16[2,512,2048]{2,1,0:T(8,128)(2,1)} collective-permute-done((bf16[2,512,2048]{2,1,0:T(8,128)(2,1)}, bf16[2,512,2048]{2,1,0:T(8,128)(2,1)}, u32[]{:S(2)}, u32[]{:S(2)}) %collective-permute-start.1) | collective-permute-done | bytes 4194336 | tf_op jit(solution)/shard_map/ppermute | solution.py:14
  215.0 4.8 slice_bitcast_fusion
  219.8 31.6 %concatenate.10 = bf16[1535,2048]{1,0:T(8,128)(2,1)} concatenate(bf16[511,2048]{1,0:T(8,128)(2,1)} %get-tuple-element.281, bf16[512,2048]{1,0:T(8,128)(2,1)} %get-tuple-element.223, bf16[512,2048]{1,0:T(8,128)(2,1)S(1)} %bitcast.154), dimensions={0} | concatenate | bytes 12574720 | tf_op jit(solution)/shard_map/concatenate | solution.py:117
  251.4 33.6 %concatenate.9 = bf16[1535,2048]{1,0:T(8,128)(2,1)} concatenate(bf16[511,2048]{1,0:T(8,128)(2,1)} %get-tuple-element.282, bf16[512,2048]{1,0:T(8,128)(2,1)} %get-tuple-element.224, bf16[512,2048]{1,0:T(8,128)(2,1)} %bitcast.155), dimensions={0} | concatenate | bytes 12574720 | tf_op jit(solution)/shard_map/concatenate | solution.py:116
  285.0 110.0 %while.28 = (s32[]{:T(128)}, bf16[16,512,128]{2,1,0:T(8,128)(2,1)S(1)}, s32[16]{0:T(128)S(1)}, bf16[512,2048]{1,0:T(8,128)(2,1)}, bf16[1535,2048]{1,0:T(8,128)(2...) while((s32[]{:T(128)}, ...), condition=%wide.region_3.4_spmd.clone, body=%wide.region_0.3_spmd.clone.sunk | while | flops 419745792 | bytes 10504381 | solution.py:135
  400.4 6.0 stack.20
  406.4 9.0 all-to-all-start
  423.8 5.8 select_select_fusion.1
  429.6 4.3 compare_select_fusion.12
  434.1 5.8 select_select_fusion
  439.9 4.3 compare_select_fusion.11
  444.3 5.4 fusion.51
  451.9 214.3 %all-to-all-done = bf16[16,256,2048]{2,1,0:T(8,128)(2,1)} async-done(((bf16[16,256,2048]{2,1,0:T(8,128)(2,1)}), bf16[16,256,2048]{2,1,0:T(8,128)(2,1)}, u32[]{:S(2)}, u32[]{:S(2)}) %all-to-all-start) | async-done | bytes 16777248 | tf_op jit(solution)/shard_map/all_to_all | solution.py:161
  666.2 24.3 %gather_fusion.3 = bf16[2048,2048]{1,0:T(8,128)(2,1)} fusion(bf16[4096,2048]{1,0:T(8,128)(2,1)} %bitcast.49, s32[2048]{0:T(1024)S(1)} %broadcast_clamp_fusion), kind=kCustom, calls=%fused_computation.3 | custom fusion | bytes 16785408 | tf_op jit(solution)/shard_map/gather | solution.py:176
  690.4 13.7 %convolution_convert_fusion.2 = bf16[4096,384]{1,0:T(8,128)(2,1)} fusion(bf16[4096,2048]{1,0:T(8,128)(2,1)} %bitcast.49, bf16[2048,128]{1,0:T(8,128)(2,1)S(1)} %get-tuple-element.231, bf16[2048,128]{1,0:T(8,128)(2,1)} %get-tuple-element.232, bf16[2048,128]{1,0:T(8,128)(2,1)S(1)} %get-tuple-element.230), kind=kOutput, calls=%fused_computation.52 | convolution fusion | flops 6448742400 | bytes 21495808 | tf_op jit(solution)/shard_map/dot_general | solution.py:170
  704.1 11.2 %gather_fusion.2 = bf16[2048,384]{1,0:T(8,128)(2,1)} fusion(bf16[4096,384]{1,0:T(8,128)(2,1)} %convolution_convert_fusion.2, s32[2048]{0:T(1024)S(1)} %broadcast_clamp_fusion), kind=kCustom, calls=%fused_computation.2 | custom fusion | bytes 3153920 | tf_op jit(solution)/shard_map/gather | solution.py:177
  717.5 50.0 %while.29 = (s32[]{:T(128)}, f32[2048,128]{1,0:T(8,128)S(1)}, f32[2048,128]{1,0:T(8,128)S(1)}, bf16[4,512,128]{2,1,0:T(8,128)(2,1)}, bf16[4,512,128]{2,1,0:T(8,1...) while((s32[]{:T(128)}, f32[2048,128]{1,0:T(8,128)S(1)}, ...), condition=%wide.region_13.14_spmd.clone, body=%wide.region_9.13_spmd.clone.sunk | while | flops 1636956672 | bytes 55361836 | solution.py:84
  767.5 9.1 %fusion.47 = f32[2048,2048]{1,0:T(8,128)} fusion(f32[2048,128]{1,0:T(8,128)S(1)} %get-tuple-element.106, bf16[3,2048,128]{2,1,0:T(8,128)(2,1)} %param.16), kind=kOutput, calls=%fused_computation.82 | convolution fusion | flops 1074003968 | bytes 18350080 | tf_op jit(solution)/shard_map/dot_general | solution.py:205
  776.6 5.9 fusion.36
  782.5 5.9 fusion.35
  788.4 9.3 %fusion.62 = f32[2048,2048]{1,0:T(8,128)} fusion(bf16[2048,128]{1,0:T(8,128)(2,1)S(1)} %bitcast.159, bf16[3,2048,128]{2,1,0:T(8,128)(2,1)} %param.16), kind=kOutput, calls=%fused_computation.172 | convolution fusion | flops 1073741824 | bytes 17825792 | tf_op jit(solution)/shard_map/dot_general | solution.py:205
  801.7 15.7 %add_convert_fusion = bf16[2048,2048]{1,0:T(8,128)(2,1)} fusion(f32[2048,2048]{1,0:T(8,128)} %fusion.62, f32[2048,2048]{1,0:T(8,128)} %fusion.47, f32[2048,128]{1,0:T(8,128)S(1)} %get-tuple-element.107, bf16[3,2048,128]{2,1,0:T(8,128)(2,1)} %param.16), kind=kOutput, calls=%fused_computation.51 | convolution fusion | flops 1086586880 | bytes 43515904 | tf_op jit(solution)/shard_map/dot_general | solution.py:205
  821.7 4.2 broadcast_in_dim_reshape.7
  825.9 37.7 %all-reduce.2.cloned.1.call-done = bf16[3,2048,128]{2,1,0:T(8,128)(2,1)} async-done(((bf16[3,2048,128]{2,1,0:T(8,128)(2,1)}), bf16[3,2048,128]{2,1,0:T(8,128)(2,1)}) %all-reduce.2.cloned.1.call-update) | async-done | bytes 1572880 | tf_op jit(solution)/shard_map/psum | solution.py:201
  867.0 33.6 %reduce-scatter.2.cloned.1.call-done = bf16[128,2048]{1,0:T(8,128)(2,1)} async-done(((bf16[2048,2048]{1,0:T(8,128)(2,1)}), bf16[128,2048]{1,0:T(8,128)(2,1)}) %reduce-scatter.2.cloned.1.call-update) | async-done | bytes 524304 | tf_op jit(solution)/shard_map/reduce_scatter | solution.py:211
  (200 shorter events, 187.5 us)
Async XLA Ops:
  10.1 3.3 copy-start.1
  19.1 18.0 %copy-start.2 = (bf16[1,512,2048]{2,1,0:T(8,128)(2,1)S(1)}, bf16[1,512,2048]{2,1,0:T(8,128)(2,1)}, u32[]{:S(2)}) copy-start(bf16[1,512,2048]{2,1,0:T(8,128)(2,1)} %param.12) | copy-start | bytes 6291460
  30.0 14.1 %copy-start = (s32[1,16]{1,0:T(1,128)S(1)}, s32[1,16]{1,0:T(1,128)}, u32[]{:S(2)}) copy-start(s32[1,16]{1,0:T(1,128)} %param.14) | copy-start | bytes 196
  30.0 96.3 %collective-permute-start = (bf16[2,511,2048]{2,0,1:T(2,128)(2,1)}, bf16[2,511,2048]{2,0,1:T(2,128)(2,1)}, u32[]{:S(2)}, u32[]{:S(2)}) collective-permute-start(bf16[2,511,2048]{2,0,1:T(2,128)(2,1)} %pad_maximum_fusion.1), channel_id=1, source_target_pairs={{0,16},{8,24},{16,32},{24,40},{32,48},{40,56},{48,64},{56,72},{64,... | collective-permute-start | bytes 12558344 | tf_op jit(solution)/shard_map/ppermute | solution.py:14
  39.4 175.6 %collective-permute-start.1 = (bf16[2,512,2048]{2,1,0:T(8,128)(2,1)}, bf16[2,512,2048]{2,1,0:T(8,128)(2,1)}, u32[]{:S(2)}, u32[]{:S(2)}) collective-permute-start(bf16[2,512,2048]{2,1,0:T(8,128)(2,1)} %pad_maximum_fusion), channel_id=1, source_target_pairs={{0,8},{8,16},{16,24},{24,32},{32,40},{40,48},{48,56},{56,64},{64,7... | collective-permute-start | bytes 12582920 | tf_op jit(solution)/shard_map/ppermute | solution.py:14
  251.4 33.6 %copy-start.3 = (bf16[16,512,128]{2,1,0:T(8,128)(2,1)S(1)}, bf16[16,512,128]{2,1,0:T(8,128)(2,1)}, u32[]{:S(2)}) copy-start(bf16[16,512,128]{2,1,0:T(8,128)(2,1)} %custom-call.10) | copy-start | bytes 6291460
  395.0 1.3 copy-start.4
  406.4 9.1 copy-start.9
  406.4 259.8 %all-to-all-start = ((bf16[16,256,2048]{2,1,0:T(8,128)(2,1)}), bf16[16,256,2048]{2,1,0:T(8,128)(2,1)}, u32[]{:S(2)}, u32[]{:S(2)}) async-start(bf16[16,256,2048]{2,1,0:T(8,128)(2,1)} %stack.20), calls=%async_computation | async-start | bytes 33554432 | tf_op jit(solution)/shard_map/all_to_all | solution.py:161
  415.4 448.2 %all-reduce.2.cloned.1.call-start = ((), (), s32[]{:S(2)}) async-start(), calls=%async_computation.2 | async-start | bytes 3145728 | tf_op jit(solution)/shard_map/psum | solution.py:201
  721.1 1.2 copy-start.6
  724.1 1.0 copy-start.8
  733.4 1.2 copy-start.6
  736.4 1.0 copy-start.8
  745.8 1.2 copy-start.6
  748.8 1.0 copy-start.8
  758.1 1.2 copy-start.6
  761.1 1.0 copy-start.8
  776.6 5.9 copy-start.7
  782.4 15.2 %slice-start = ((s8[8388608]{0:T(1024)(128)(4,1)}), s8[4194304]{0:T(1024)(128)(4,1)S(1)}, s32[]{:S(2)}) async-start(s8[8388608]{0:T(1024)(128)(4,1)} %bitcast.152), calls=%async_computation.4 | async-start | bytes 8388608
  788.4 9.3 %slice-start.1 = ((s8[8388608]{0:T(1024)(128)(4,1)}), s8[4194304]{0:T(1024)(128)(4,1)S(1)}, s32[]{:S(2)}) async-start(s8[8388608]{0:T(1024)(128)(4,1)} %bitcast.152), calls=%async_computation.5 | async-start | bytes 8388608
  801.6 99.0 %reduce-scatter.2.cloned.1.call-start = ((), (), s32[]{:S(2)}) async-start(), calls=%async_computation.3 | async-start | bytes 8912896 | tf_op jit(solution)/shard_map/reduce_scatter | solution.py:211
  817.4 1.6 copy-start.5
Sparse Core Ops, SparseCore 0:
  801.8 61.7 all-reduce.1
Sparse Core Ops, SparseCore 1:
  817.5 83.0 reduce-scatter.1
